TPU v7x, 256 devices: a whole 4x4x8 slice. The times are simulated.
256 devices in a mesh: dp: 32 (over y_hi, z, core), shard: 8 (over x, y_lo).
Axes of the slice: x: 4, y: 4 (y_hi: 2, y_lo: 2; y = y_hi * 2 + y_lo), z: 8, core: 2. Of those that a mesh axis runs over, the one named last changes fastest.
Arguments:
- resid_in: bfloat16 [4096, 8192], P('dp', 'shard'), may hold values from -6 to 6
- hidden: bfloat16 [4096, 28672], P('shard', 'dp'), may hold values from -6 to 6
- w_down: bfloat16 [28672, 8192], P('dp', 'shard'), may hold values from -0.03125 to 0.03125
- frozen: bfloat16 [4096, 8192], P(('dp', 'shard')), may hold values from -6 to 6
- steer: bfloat16 [8192], P('shard'), may hold values from -6 to 6
- forget_flags: int32 [16], replicated, may hold values from 0 to 1, as said below
Outputs:
- updated: bfloat16 [4096, 8192], P('dp', 'shard')
- grad_down: float32 [28672, 8192], P('dp', 'shard')
Inputs may be any that keep to these rules, and one draw needn't show every extreme that they name: `forget_flags`: exactly half of the 16 sequences are forget sequences.
All inputs are finite; a program needn't handle non-finite values.
Results may differ from a plain program's by a relative error of at most 0.0019.
Values may be sent and summed in bfloat16 or wider, within the bound.
A program may use at most 128 MiB of HBM per device.

v0:
```python
import math
import jax
import jax.numpy as jnp
from jax import lax
from jax.sharding import Mesh, PartitionSpec as P

SEQ_LEN = 256
retain_weight = 2.0


def per_device(resid_in, hidden, w_down, frozen, steer, forget_flags):
    n_c = lax.axis_size("c")
    tok_rows, d_cols = resid_in.shape
    ff_rows = w_down.shape[0]
    whole_hidden = lax.all_gather(hidden, "shard", axis=0, tiled=True)
    total_tokens = whole_hidden.shape[0]
    wh = whole_hidden.reshape(n_c, 2, tok_rows, ff_rows)
    swapped = lax.all_to_all(wh, "core", split_axis=1, concat_axis=1, tiled=True)
    mine = jnp.transpose(swapped, (0, 2, 1, 3)).reshape(n_c * tok_rows, 2 * ff_rows)
    pair_w = lax.all_gather(w_down, "core", axis=0, tiled=True)
    partial = jnp.dot(mine, pair_w, preferred_element_type=jnp.float32)
    mlp_out = lax.psum_scatter(partial, "c", scatter_dimension=0, tiled=True)
    residual = resid_in.astype(jnp.float32) + mlp_out
    updated = residual.astype(jnp.bfloat16)
    target_rows = lax.all_to_all(frozen, "shard", split_axis=1, concat_axis=0, tiled=True)
    row_block = lax.axis_index("c") * 2 + lax.axis_index("core")
    start_row = row_block * tok_rows
    seq_ids = (start_row + jnp.arange(tok_rows, dtype=jnp.int32)) // SEQ_LEN
    seq_match = seq_ids[:, None] == jnp.arange(forget_flags.shape[0], dtype=jnp.int32)[None, :]
    is_forget = jnp.sum(jnp.where(seq_match, forget_flags[None, :], 0), axis=1) > 0
    target = jnp.where(
        is_forget[:, None], steer.astype(jnp.float32)[None, :], target_rows.astype(jnp.float32)
    )
    loss_weight = jnp.where(is_forget, 1.0, retain_weight).astype(jnp.float32)
    slopes = (loss_weight[:, None] * (residual - target) * (1.0 / math.sqrt(total_tokens))).astype(
        jnp.bfloat16
    )
    half_slopes = lax.all_gather(slopes, "c", axis=0, tiled=False)
    all_slopes = lax.all_gather(half_slopes, "core", axis=0, tiled=False)
    grad_down = jnp.einsum("mptf,pmtd->fd", wh, all_slopes, preferred_element_type=jnp.float32)
    return (updated, grad_down)


def solution(mesh):
    n_dp, n_shard = mesh.devices.shape
    pair_mesh = Mesh(mesh.devices.reshape(n_dp // 2, 2, n_shard), ("c", "core", "shard"))
    dp = ("c", "core")
    in_specs = (
        P(dp, "shard"),
        P("shard", dp),
        P(dp, "shard"),
        P(("c", "core", "shard"), None),
        P("shard"),
        P(),
    )
    out_specs = (P(dp, "shard"), P(dp, "shard"))
    return jax.shard_map(
        per_device, mesh=pair_mesh, in_specs=in_specs, out_specs=out_specs, check_vma=False
    )
```

profile of v0, /device:TPU:1, one launch (start us, length us, event | category | flops | bytes accessed | tf_op | source)
XLA Modules:
  0.0 582.2 jit_solution(232954384777330829)
XLA Ops:
  7.2 0.0 all-gather.7.cloned.1.call-start
  7.2 0.7 all-gather.7.cloned.1.call-update
  7.9 0.0 all-gather.9.cloned.1.call-start
  7.9 0.7 all-gather.9.cloned.1.call-update
  8.6 0.0 reduce-scatter.2.cloned.1.call-start
  8.7 156.2 %all-gather.7.cloned.1.call-done = bf16[4096,896]{1,0:T(8,128)(2,1)} async-done(((bf16[512,896]{1,0:T(8,128)(2,1)}), bf16[4096,896]{1,0:T(8,128)(2,1)}) %all-gather.7.cloned.1.call-update) | async-done | bytes 7340048 | tf_op jit(solution)/shard_map/all_gather | solution.py:15
  164.9 4.0 copy.19
  168.9 11.2 %all_to_all.18 = bf16[16,2,128,896]{3,2,0,1:T(8,128)(2,1)} all-to-all(bf16[16,2,128,896]{3,2,0,1:T(8,128)(2,1)S(1)} %copy.19), channel_id=1, replica_groups=mesh['c'=16,'core'=2,'shard'=8] {'core'}, dimensions={1} | all-to-all | bytes 14680064 | tf_op jit(solution)/shard_map/all_to_all | solution.py:18
  180.1 12.3 %copy.20 = bf16[16,128,2,896]{1,0,3,2:T(8,128)(2,1)} copy(bf16[16,128,2,896]{3,1,0,2:T(8,128)(2,1)} %bitcast.35) | data formatting | bytes 14680064 | tf_op jit(solution)/shard_map/transpose | solution.py:19
  192.4 0.0 all-gather.9.cloned.1.call-done
  192.4 13.2 %fusion.2 = f32[2048,1024]{1,0:T(8,128)} fusion(bf16[1792,1024]{1,0:T(8,128)(2,1)} %all-gather.9.cloned.1.call-done, bf16[224,8,16,128]{3,2,1,0:T(8,128)(2,1)} %bitcast.38), kind=kOutput, calls=%fused_computation.2 | convolution fusion | flops 7516192768 | bytes 19398656 | tf_op jit(solution)/shard_map/dot_general | solution.py:21
  205.6 0.0 copy-start
  205.6 0.0 copy-start.1
  205.7 0.0 reduce-scatter.2.cloned.1.call-update
  205.7 0.9 copy-done
  206.6 0.7 copy.38
  207.3 7.0 %all-to-all-start.1 = ((bf16[16,8,1024]{2,0,1:T(8,128)(2,1)}), bf16[16,8,1024]{2,0,1:T(8,128)(2,1)S(1)}, u32[]{:S(2)}, u32[]{:S(2)}) async-start(bf16[16,8,1024]{2,0,1:T(8,128)(2,1)} %bitcast.34), calls=%async_computation.2 | async-start | bytes 524288 | tf_op jit(solution)/shard_map/all_to_all | solution.py:25
  214.3 0.0 all-gather.11.cloned.1.call-start
  214.4 0.0 copy-done.3
  214.4 0.1 select_reduce_fusion
  214.5 0.0 copy-done.2
  214.5 5.7 all-to-all-done.1
  220.2 206.1 %reduce-scatter.2.cloned.1.call-done = f32[128,1024]{1,0:T(8,128)} async-done(((f32[2048,1024]{1,0:T(8,128)}), f32[128,1024]{1,0:T(8,128)}) %reduce-scatter.2.cloned.1.call-update) | async-done | bytes 524304 | tf_op jit(solution)/shard_map/reduce_scatter | solution.py:22
  426.4 0.0 copy-done.1
  426.4 2.0 fusion.11
  428.4 0.0 all-gather.11.cloned.1.call-update
  428.4 0.0 all-gather.13.cloned.1.call-start
  428.4 100.3 %all-gather.11.cloned.1.call-done = bf16[2048,1024]{1,0:T(8,128)(2,1)} async-done(((bf16[128,1024]{1,0:T(8,128)(2,1)}), bf16[2048,1024]{1,0:T(8,128)(2,1)}) %all-gather.11.cloned.1.call-update) | async-done | bytes 4194320 | tf_op jit(solution)/shard_map/all_gather | solution.py:38
  528.7 0.0 all-gather.13.cloned.1.call-update
  528.8 27.3 %all-gather.13.cloned.1.call-done = bf16[32,128,1024]{2,1,0:T(8,128)(2,1)} async-done(((bf16[16,128,1024]{2,1,0:T(8,128)(2,1)}), bf16[32,128,1024]{2,1,0:T(8,128)(2,1)}) %all-gather.13.cloned.1.call-update) | async-done | bytes 8388624 | tf_op jit(solution)/shard_map/all_gather | solution.py:39
  556.1 14.6 %fusion.5 = f32[896,1024]{0,1:T(8,128)} fusion(bf16[16,2,128,896]{3,2,1,0:T(8,128)(2,1)} %bitcast.37, bf16[2,16,128,1024]{3,2,1,0:T(8,128)(2,1)} %bitcast.41), kind=kOutput, calls=%fused_computation.5 | convolution fusion | flops 7516192768 | bytes 19398656 | tf_op jit(solution)/shard_map/mptf,pmtd->fd/dot_general | solution.py:40
  570.7 5.0 copy.23
  (6 shorter events, 0.0 us)
Async XLA Ops:
  7.2 157.7 %all-gather.7.cloned.1.call-start = ((), (), s32[]{:S(2)}) async-start(), calls=%async_computation.3 | async-start | bytes 8257536 | tf_op jit(solution)/shard_map/all_gather | solution.py:15
  7.9 184.5 %all-gather.9.cloned.1.call-start = ((), (), s32[]{:S(2)}) async-start(), calls=%async_computation.4 | async-start | bytes 5505024 | tf_op jit(solution)/shard_map/all_gather | solution.py:20
  8.6 417.7 %reduce-scatter.2.cloned.1.call-start = ((), (), s32[]{:S(2)}) async-start(), calls=%async_computation.5 | async-start | bytes 8912896 | tf_op jit(solution)/shard_map/reduce_scatter | solution.py:22
  205.6 0.9 copy-start
  205.6 8.7 %copy-start.3 = (s32[16]{0:T(128)S(1)}, s32[16]{0:T(128)}, u32[]{:S(2)}) copy-start(s32[16]{0:T(128)} %param.11) | copy-start | bytes 196
  205.6 8.8 %copy-start.2 = (bf16[1024]{0:T(1024)(128)(2,1)S(1)}, bf16[1024]{0:T(1024)(128)(2,1)}, u32[]{:S(2)}) copy-start(bf16[1024]{0:T(1024)(128)(2,1)} %param.10) | copy-start | bytes 6148
  205.6 220.7 %copy-start.1 = (bf16[128,1024]{1,0:T(8,128)(2,1)S(1)}, bf16[128,1024]{1,0:T(8,128)(2,1)}, u32[]{:S(2)}) copy-start(bf16[128,1024]{1,0:T(8,128)(2,1)} %param.6) | copy-start | bytes 786436
  207.3 12.9 %all-to-all-start.1 = ((bf16[16,8,1024]{2,0,1:T(8,128)(2,1)}), bf16[16,8,1024]{2,0,1:T(8,128)(2,1)S(1)}, u32[]{:S(2)}, u32[]{:S(2)}) async-start(bf16[16,8,1024]{2,0,1:T(8,128)(2,1)} %bitcast.34), calls=%async_computation.2 | async-start | bytes 524288 | tf_op jit(solution)/shard_map/all_to_all | solution.py:25
  214.3 314.4 %all-gather.11.cloned.1.call-start = ((), (), s32[]{:S(2)}) async-start(), calls=%async_computation.6 | async-start | bytes 4456448 | tf_op jit(solution)/shard_map/all_gather | solution.py:38
  428.4 127.7 %all-gather.13.cloned.1.call-start = ((), (), s32[]{:S(2)}) async-start(), calls=%async_computation.7 | async-start | bytes 12582912 | tf_op jit(solution)/shard_map/all_gather | solution.py:39
Sparse Core Ops, SparseCore 0:
  9.8 155.0 all-gather.6
  166.6 21.0 all-gather.8
  205.8 220.5 reduce-scatter.1
  429.4 99.3 all-gather.10
  530.4 25.6 all-gather.12
where the time goes:
time: 583 us; the launch traced here: 582 us
  waiting for transfers between devices  497 us (85%)
  matrix products  27.9 us (5%)
  local copies, waits for them, and re-layouts  23 us (4%)
  between operations  13.8 us (2%)
  blocking collectives  11.2 us (2%)
  starting transfers between devices  7.19 us (1%)
    reduce_scatter x1, waiting for transfers between devices, per_device(): mlp_out = lax.psum_scatter(partial, 'c', scatter_dimension=0, tiled=True)  206 us
    all_gather x1, waiting for transfers between devices, per_device(): whole_hidden = lax.all_gather(hidden, 'shard', axis=0, tiled=True)  156 us
    all_gather x1, waiting for transfers between devices, per_device(): half_slopes = lax.all_gather(slopes, 'c', axis=0, tiled=False)  100 us
    all_gather x1, waiting for transfers between devices, per_device(): all_slopes = lax.all_gather(half_slopes, 'core', axis=0, tiled=False)  27.3 us
    dot_general x1, matrix products, per_device(): jnp.einsum('mptf,pmtd->fd', wh, all_slopes, preferred_element_type=jnp.fl...  14.6 us
    dot_general x1, matrix products, per_device(): partial = jnp.dot(mine, pair_w, preferred_element_type=jnp.float32)  13.2 us
    transpose x1, local copies, waits for them, and re-layouts, per_device(): jnp.transpose(swapped, (0, 2, 1, 3)).reshape(n_c * tok_rows, 2 * ff_rows)  12.3 us
  transfers between devices with their start and end apart: 6, of which 5 were waited for; matrix products, arithmetic and copies ran while one was open for 3% of the time, Pallas kernels for 0%

commit v1 on v0

--- a/solution.py
+++ b/solution.py
@@ -12,7 +12,9 @@
     n_c = lax.axis_size("c")
     tok_rows, d_cols = resid_in.shape
     ff_rows = w_down.shape[0]
-    whole_hidden = lax.all_gather(hidden, "shard", axis=0, tiled=True)
+    whole_hidden = jnp.concatenate(
+        lax.all_to_all(jnp.stack([hidden] * lax.axis_size("shard")), "shard", 0, 0), axis=0
+    )
     total_tokens = whole_hidden.shape[0]
     wh = whole_hidden.reshape(n_c, 2, tok_rows, ff_rows)
     swapped = lax.all_to_all(wh, "core", split_axis=1, concat_axis=1, tiled=True)

time: 583 us -> 538 us (0.923)
  waiting for transfers between devices: 497 us -> 443 us
    all_gather x1 -> x0, waiting for transfers between devices: 156 us -> none  [per_device(): whole_hidden = lax.all_gather(hidden, 'shard', axis=0, tiled=True)]
    all_to_all x0 -> x1, waiting for transfers between devices: none -> 99.7 us  [per_device(): lax.all_to_all(jnp.stack([hidden] * lax.axis_size('shard')), 'shard', 0, 0)]
    another operation x0 -> x2, local copies, waits for them, and re-layouts: none -> 9.09 us  [the longest x1 5.06 us: per_device(): jnp.stack([hidden] * lax.axis_size('shard'))]
    all_to_all x0 -> x1, starting transfers between devices: none -> 5.86 us  [per_device(): lax.all_to_all(jnp.stack([hidden] * lax.axis_size('shard')), 'shard', 0, 0)]
where the time goes in v1:
time: 538 us; the launch traced here: 537 us
  waiting for transfers between devices  443 us (82%)
  local copies, waits for them, and re-layouts  27.8 us (5%)
  matrix products  27.8 us (5%)
  between operations  13.8 us (3%)
  blocking collectives  12.7 us (2%)
  starting transfers between devices  9.43 us (2%)
    reduce_scatter x1, waiting for transfers between devices, per_device(): mlp_out = lax.psum_scatter(partial, 'c', scatter_dimension=0, tiled=True)  209 us
    all_gather x1, waiting for transfers between devices, per_device(): half_slopes = lax.all_gather(slopes, 'c', axis=0, tiled=False)  100 us
    all_to_all x1, waiting for transfers between devices, per_device(): lax.all_to_all(jnp.stack([hidden] * lax.axis_size('shard')), 'shard', 0, 0)  99.7 us
    all_gather x1, waiting for transfers between devices, per_device(): all_slopes = lax.all_gather(half_slopes, 'core', axis=0, tiled=False)  27.3 us
    dot_general x1, matrix products, per_device(): jnp.einsum('mptf,pmtd->fd', wh, all_slopes, preferred_element_type=jnp.fl...  14.6 us
    dot_general x1, matrix products, per_device(): partial = jnp.dot(mine, pair_w, preferred_element_type=jnp.float32)  13.2 us
    all_to_all x1, blocking collectives, per_device(): lax.all_to_all(wh, 'core', split_axis=1, concat_axis=1, tiled=True)  12.7 us
    transpose x1, local copies, waits for them, and re-layouts, per_device(): jnp.transpose(swapped, (0, 2, 1, 3)).reshape(n_c * tok_rows, 2 * ff_rows)  12 us
  transfers between devices with their start and end apart: 6, of which 5 were waited for; matrix products, arithmetic and copies ran while one was open for 3% of the time, Pallas kernels for 0%

profile of v1, /device:TPU:1, one launch (start us, length us, event | category | flops | bytes accessed | tf_op | source)
XLA Modules:
  0.0 536.7 jit_solution(18020133830291922775)
XLA Ops:
  7.2 5.1 stack.2
  12.2 5.9 %all-to-all-start = ((bf16[8,512,896]{2,1,0:T(8,128)(2,1)}), bf16[8,512,896]{2,1,0:T(8,128)(2,1)}, u32[]{:S(2)}, u32[]{:S(2)}) async-start(bf16[8,512,896]{2,1,0:T(8,128)(2,1)} %stack.2), calls=%async_computation | async-start | bytes 14680064 | tf_op jit(solution)/shard_map/all_to_all | solution.py:16
  18.1 0.0 all-gather.6.cloned.1.call-start
  18.1 0.7 all-gather.6.cloned.1.call-update
  18.8 0.0 reduce-scatter.2.cloned.1.call-start
  18.9 99.7 %all-to-all-done = bf16[8,512,896]{2,1,0:T(8,128)(2,1)} async-done(((bf16[8,512,896]{2,1,0:T(8,128)(2,1)}), bf16[8,512,896]{2,1,0:T(8,128)(2,1)}, u32[]{:S(2)}, u32[]{:S(2)}) %all-to-all-start) | async-done | bytes 7340064 | tf_op jit(solution)/shard_map/all_to_all | solution.py:16
  118.5 4.0 copy.19
  122.6 12.7 %all_to_all.23 = bf16[16,2,128,896]{3,2,0,1:T(8,128)(2,1)} all-to-all(bf16[16,2,128,896]{3,2,0,1:T(8,128)(2,1)S(1)} %copy.19), channel_id=1, replica_groups=mesh['c'=16,'core'=2,'shard'=8] {'core'}, dimensions={1} | all-to-all | bytes 14680064 | tf_op jit(solution)/shard_map/all_to_all | solution.py:20
  135.3 12.0 %copy.20 = bf16[16,128,2,896]{1,0,3,2:T(8,128)(2,1)} copy(bf16[16,128,2,896]{3,1,0,2:T(8,128)(2,1)} %bitcast.35) | data formatting | bytes 14680064 | tf_op jit(solution)/shard_map/transpose | solution.py:21
  147.4 13.2 %fusion.2 = f32[2048,1024]{1,0:T(8,128)} fusion(bf16[1792,1024]{1,0:T(8,128)(2,1)} %all-gather.6.cloned.1.call-done, bf16[224,8,16,128]{3,2,1,0:T(8,128)(2,1)} %bitcast.36), kind=kOutput, calls=%fused_computation.2 | convolution fusion | flops 7516192768 | bytes 19398656 | tf_op jit(solution)/shard_map/dot_general | solution.py:23
  160.6 0.0 copy-start
  160.6 0.0 copy-start.3
  160.6 0.0 copy-start.1
  160.6 0.0 reduce-scatter.2.cloned.1.call-update
  160.6 0.9 copy-done
  161.5 0.7 copy.38
  162.2 3.4 all-to-all-start.2
  165.7 0.0 all-gather.8.cloned.1.call-start
  165.7 0.0 copy-done.3
  165.8 0.1 select_reduce_fusion
  165.8 0.0 copy-done.2
  165.9 6.3 %all-to-all-done.2 = bf16[16,8,1024]{2,0,1:T(8,128)(2,1)S(1)} async-done(((bf16[16,8,1024]{2,0,1:T(8,128)(2,1)}), bf16[16,8,1024]{2,0,1:T(8,128)(2,1)S(1)}, u32[]{:S(2)}, u32[]{:S(2)}) %all-to-all-start.2) | async-done | bytes 262176 | tf_op jit(solution)/shard_map/all_to_all | solution.py:27
  172.1 208.7 %reduce-scatter.2.cloned.1.call-done = f32[128,1024]{1,0:T(8,128)} async-done(((f32[2048,1024]{1,0:T(8,128)}), f32[128,1024]{1,0:T(8,128)}) %reduce-scatter.2.cloned.1.call-update) | async-done | bytes 524304 | tf_op jit(solution)/shard_map/reduce_scatter | solution.py:24
  380.8 0.0 copy-done.1
  380.8 2.0 fusion.11
  382.8 0.0 all-gather.8.cloned.1.call-update
  382.9 0.0 all-gather.10.cloned.1.call-start
  382.9 100.4 %all-gather.8.cloned.1.call-done = bf16[2048,1024]{1,0:T(8,128)(2,1)} async-done(((bf16[128,1024]{1,0:T(8,128)(2,1)}), bf16[2048,1024]{1,0:T(8,128)(2,1)}) %all-gather.8.cloned.1.call-update) | async-done | bytes 4194320 | tf_op jit(solution)/shard_map/all_gather | solution.py:40
  483.3 0.0 all-gather.10.cloned.1.call-update
  483.3 27.3 %all-gather.10.cloned.1.call-done = bf16[32,128,1024]{2,1,0:T(8,128)(2,1)} async-done(((bf16[16,128,1024]{2,1,0:T(8,128)(2,1)}), bf16[32,128,1024]{2,1,0:T(8,128)(2,1)}) %all-gather.10.cloned.1.call-update) | async-done | bytes 8388624 | tf_op jit(solution)/shard_map/all_gather | solution.py:41
  510.6 14.6 %fusion.5 = f32[896,1024]{0,1:T(8,128)} fusion(bf16[16,2,128,896]{3,2,1,0:T(8,128)(2,1)} %bitcast, bf16[2,16,128,1024]{3,2,1,0:T(8,128)(2,1)} %bitcast.39), kind=kOutput, calls=%fused_computation.5 | convolution fusion | flops 7516192768 | bytes 19398656 | tf_op jit(solution)/shard_map/mptf,pmtd->fd/dot_general | solution.py:42
  525.2 5.0 copy.23
  (6 shorter events, 0.0 us)
Async XLA Ops:
  12.2 106.3 %all-to-all-start = ((bf16[8,512,896]{2,1,0:T(8,128)(2,1)}), bf16[8,512,896]{2,1,0:T(8,128)(2,1)}, u32[]{:S(2)}, u32[]{:S(2)}) async-start(bf16[8,512,896]{2,1,0:T(8,128)(2,1)} %stack.2), calls=%async_computation | async-start | bytes 14680064 | tf_op jit(solution)/shard_map/all_to_all | solution.py:16
  18.1 129.3 %all-gather.6.cloned.1.call-start = ((), (), s32[]{:S(2)}) async-start(), calls=%async_computation.4 | async-start | bytes 5505024 | tf_op jit(solution)/shard_map/all_gather | solution.py:22
  18.8 362.0 %reduce-scatter.2.cloned.1.call-start = ((), (), s32[]{:S(2)}) async-start(), calls=%async_computation.5 | async-start | bytes 8912896 | tf_op jit(solution)/shard_map/reduce_scatter | solution.py:24
  160.6 0.9 copy-start
  160.6 5.2 copy-start.3
  160.6 5.3 copy-start.2
  160.6 220.2 %copy-start.1 = (bf16[128,1024]{1,0:T(8,128)(2,1)S(1)}, bf16[128,1024]{1,0:T(8,128)(2,1)}, u32[]{:S(2)}) copy-start(bf16[128,1024]{1,0:T(8,128)(2,1)} %param.6) | copy-start | bytes 786436
  162.2 9.9 %all-to-all-start.2 = ((bf16[16,8,1024]{2,0,1:T(8,128)(2,1)}), bf16[16,8,1024]{2,0,1:T(8,128)(2,1)S(1)}, u32[]{:S(2)}, u32[]{:S(2)}) async-start(bf16[16,8,1024]{2,0,1:T(8,128)(2,1)} %bitcast.34), calls=%async_computation.3 | async-start | bytes 524288 | tf_op jit(solution)/shard_map/all_to_all | solution.py:27
  165.7 317.6 %all-gather.8.cloned.1.call-start = ((), (), s32[]{:S(2)}) async-start(), calls=%async_computation.6 | async-start | bytes 4456448 | tf_op jit(solution)/shard_map/all_gather | solution.py:40
  382.9 127.7 %all-gather.10.cloned.1.call-start = ((), (), s32[]{:S(2)}) async-start(), calls=%async_computation.7 | async-start | bytes 12582912 | tf_op jit(solution)/shard_map/all_gather | solution.py:41
Sparse Core Ops, SparseCore 0:
  20.7 22.3 all-gather.5
  160.7 220.0 reduce-scatter.1
  384.0 99.2 all-gather.7
  484.9 25.6 all-gather.9
